TPU v7x, 512 devices: a whole 4x8x8 slice. The times are simulated.
512 devices in a mesh: dp: 32 (over x_lo, y, core), head: 16 (over z, x_hi).
Axes of the slice: x: 4 (x_hi: 2, x_lo: 2; x = x_hi * 2 + x_lo), y: 8, z: 8, core: 2. Of those that a mesh axis runs over, the one named last changes fastest.
Arguments:
- hidden_in: bfloat16 [8192, 7168], P('dp', 'head'), may hold values from -6 to 6
- latent_unnormed: bfloat16 [8192, 512], P('dp'), may hold values from -6 to 6
- unrotated_key: bfloat16 [8192, 64], P('dp'), may hold values from -6 to 6
- latent_norm_scale: float32 [512], replicated, may hold values from 0.1 to 1.9
- plain_query_rows: bfloat16 [8192, 16384], P('dp', 'head'), may hold values from -6 to 6
- rotated_query_rows: bfloat16 [8192, 8192], P('dp', 'head'), may hold values from -240 to 240
- key_up_matrix: bfloat16 [512, 16384], P('dp', 'head'), may hold values from -0.25 to 0.25
- value_up_matrix: bfloat16 [512, 16384], P('dp', 'head'), may hold values from -0.25 to 0.25
- output_cotangent: bfloat16 [8192, 16384], P('dp', 'head'), may hold values from -6 to 6
- down_weight: float32 [576, 7168], P('dp', 'head'), may hold values from -0.0625 to 0.0625
- first_moment: float32 [576, 7168], P('dp', 'head'), may hold values from -0.078125 to 0.078125
- second_moment: float32 [576, 7168], P('dp', 'head'), may hold values from 4e-08 to 4e-07
Outputs:
- query_grad_nope: bfloat16 [8192, 16384], P('dp', 'head')
- query_grad_rope: bfloat16 [8192, 8192], P('dp', 'head')
- new_weight: float32 [576, 7168], P('dp', 'head')
- new_first: float32 [576, 7168], P('dp', 'head')
- new_second: float32 [576, 7168], P('dp', 'head')
All inputs are finite; a program needn't handle non-finite values.
Results may differ from a plain program's by a relative error of at most 0.011.
The roundings to bfloat16 on the way count: a program that leaves them out, or rounds other values in their place, can miss the bound.
Values may be sent and summed in bfloat16 or wider, within the bound.
A program may use at most 64 MiB of HBM per device.

v0:
```python
import math
import jax
import jax.numpy as jnp
from jax import lax
from jax.sharding import PartitionSpec as P

SEQUENCE_LENGTH = 256
norm_eps = 1e-06
beta_one = 0.9
beta_two = 0.999
adam_eps = 1e-08
learn_rate = 0.01
decay_rate = 0.1
bias_one = 1.0 - 0.9**2
bias_two = 1.0 - 0.999**2


def angle_tables(positions, rope_width):
    half_width = rope_width // 2
    inverse_freq = jnp.exp(
        jnp.arange(half_width, dtype=jnp.float32) * (-2.0 * math.log(10000.0) / rope_width)
    )
    angles = positions.astype(jnp.float32)[:, None] * inverse_freq[None, :]
    return (jnp.cos(angles), jnp.sin(angles))


def latent_back(
    latent_sum, rope_sum, latent_in, inverse_rms, latent_norm_scale, cos_table, sin_table
):
    latent_width = latent_in.shape[1]
    scaled_grad = latent_norm_scale * latent_sum
    inner_sum = jnp.sum(latent_in * scaled_grad, axis=1, keepdims=True)
    latent_grad = (
        inverse_rms * scaled_grad
        - latent_in * (inverse_rms * inverse_rms * inverse_rms) * inner_sum / latent_width
    )
    half_width = rope_sum.shape[1] // 2
    grad_first = rope_sum[:, :half_width]
    grad_second = rope_sum[:, half_width:]
    rope_grad = jnp.concatenate(
        (
            grad_first * cos_table + grad_second * sin_table,
            grad_second * cos_table - grad_first * sin_table,
        ),
        axis=1,
    )
    return jnp.concatenate((latent_grad, rope_grad), axis=1).astype(jnp.bfloat16)


def local(
    hidden_in,
    latent_unnormed,
    unrotated_key,
    latent_norm_scale,
    plain_query_rows,
    rotated_query_rows,
    key_up_matrix,
    value_up_matrix,
    output_cotangent,
    down_weight,
    first_moment,
    second_moment,
):
    row_count = latent_unnormed.shape[0]
    rope_width = unrotated_key.shape[1]
    head_count = rotated_query_rows.shape[1] // rope_width
    nope_width = plain_query_rows.shape[1] // head_count
    value_width = output_cotangent.shape[1] // head_count
    seq_count = row_count // SEQUENCE_LENGTH
    scale_factor = 1.0 / math.sqrt(nope_width + rope_width)
    positions = jnp.arange(row_count, dtype=jnp.int32) % SEQUENCE_LENGTH
    cos_table, sin_table = angle_tables(positions, rope_width)
    raw_key = unrotated_key.astype(jnp.float32)
    half_width = rope_width // 2
    first_half = raw_key[:, :half_width]
    second_half = raw_key[:, half_width:]
    key_rot = jnp.concatenate(
        (
            first_half * cos_table - second_half * sin_table,
            first_half * sin_table + second_half * cos_table,
        ),
        axis=1,
    ).astype(jnp.bfloat16)
    latent_in = latent_unnormed.astype(jnp.float32)
    inverse_rms = lax.rsqrt(jnp.mean(latent_in * latent_in, axis=1, keepdims=True) + norm_eps)
    latent = (latent_in * inverse_rms * latent_norm_scale).astype(jnp.bfloat16)
    joined = jnp.concatenate((key_up_matrix, value_up_matrix), axis=1)
    split_at = head_count * nope_width
    full_rows = lax.all_gather(joined, "dp", axis=0, tiled=True)
    projected = jnp.dot(latent, full_rows, preferred_element_type=jnp.float32)
    key_nope = (
        projected[:, :split_at]
        .astype(jnp.bfloat16)
        .reshape(seq_count, SEQUENCE_LENGTH, head_count, nope_width)
    )
    value_rows = (
        projected[:, split_at:]
        .astype(jnp.bfloat16)
        .reshape(seq_count, SEQUENCE_LENGTH, head_count, value_width)
    )
    nope_query = plain_query_rows.reshape(seq_count, SEQUENCE_LENGTH, head_count, nope_width)
    rope_query = rotated_query_rows.reshape(seq_count, SEQUENCE_LENGTH, head_count, rope_width)
    grad_rows = output_cotangent.reshape(seq_count, SEQUENCE_LENGTH, head_count, value_width)
    rot_rows = key_rot.reshape(seq_count, SEQUENCE_LENGTH, rope_width)
    scores = (
        jnp.einsum("bthd,bshd->bhts", nope_query, key_nope, preferred_element_type=jnp.float32)
        + jnp.einsum("bthd,bsd->bhts", rope_query, rot_rows, preferred_element_type=jnp.float32)
    ) * scale_factor
    causal = jnp.arange(SEQUENCE_LENGTH)[:, None] >= jnp.arange(SEQUENCE_LENGTH)[None, :]
    scores = jnp.where(causal, scores, -1e30)
    maxima = jnp.max(scores, axis=-1, keepdims=True)
    exponent = jnp.exp(scores - maxima)
    probabilities = exponent / jnp.sum(exponent, axis=-1, keepdims=True)
    prob_low = probabilities.astype(jnp.bfloat16)
    attended = jnp.einsum(
        "bhts,bshd->bthd", prob_low, value_rows, preferred_element_type=jnp.float32
    )
    delta_sum = jnp.einsum("bthd,bthd->bht", grad_rows.astype(jnp.float32), attended)
    grad_probs = jnp.einsum(
        "bthd,bshd->bhts", grad_rows, value_rows, preferred_element_type=jnp.float32
    )
    grad_scores = probabilities * (grad_probs - delta_sum[..., None]) * scale_factor
    score_low = grad_scores.astype(jnp.bfloat16)
    grad_nope_q = jnp.einsum(
        "bhts,bshd->bthd", score_low, key_nope, preferred_element_type=jnp.float32
    ).astype(jnp.bfloat16)
    grad_rope_q = jnp.einsum(
        "bhts,bsd->bthd", score_low, rot_rows, preferred_element_type=jnp.float32
    ).astype(jnp.bfloat16)
    grad_key = jnp.einsum(
        "bhts,bthd->bshd", score_low, nope_query, preferred_element_type=jnp.float32
    ).astype(jnp.bfloat16)
    grad_value = jnp.einsum(
        "bhts,bthd->bshd", prob_low, grad_rows, preferred_element_type=jnp.float32
    ).astype(jnp.bfloat16)
    rope_part = jnp.einsum(
        "bhts,bthd->bsd", score_low, rope_query, preferred_element_type=jnp.float32
    ).reshape(row_count, rope_width)
    grads_joined = jnp.concatenate(
        (
            grad_key.reshape(row_count, split_at),
            grad_value.reshape(row_count, head_count * value_width),
        ),
        axis=1,
    )
    latent_part = jnp.einsum(
        "tk,ck->tc", grads_joined, full_rows, preferred_element_type=jnp.float32
    )
    latent_sum, rope_sum = lax.psum((latent_part, rope_part), "head")
    kv_grad = latent_back(
        latent_sum, rope_sum, latent_in, inverse_rms, latent_norm_scale, cos_table, sin_table
    )
    weight_sum = lax.psum_scatter(
        jnp.einsum("tc,td->cd", kv_grad, hidden_in, preferred_element_type=jnp.float32),
        "dp",
        scatter_dimension=0,
        tiled=True,
    )
    weight_grad = weight_sum / (row_count * lax.axis_size("dp"))
    new_first = beta_one * first_moment + (1.0 - beta_one) * weight_grad
    new_second = beta_two * second_moment + (1.0 - beta_two) * weight_grad * weight_grad
    direction = new_first / bias_one / (jnp.sqrt(new_second / bias_two) + adam_eps)
    new_weight = down_weight - learn_rate * (direction + decay_rate * down_weight)
    return (
        grad_nope_q.reshape(row_count, split_at),
        grad_rope_q.reshape(row_count, head_count * rope_width),
        new_weight,
        new_first,
        new_second,
    )


def solution(mesh):
    placed = (
        P("dp", "head"),
        P("dp", None),
        P("dp", None),
        P(),
        P("dp", "head"),
        P("dp", "head"),
        P("dp", "head"),
        P("dp", "head"),
        P("dp", "head"),
        P("dp", "head"),
        P("dp", "head"),
        P("dp", "head"),
    )
    return jax.shard_map(
        local,
        mesh=mesh,
        in_specs=placed,
        out_specs=(
            P("dp", "head"),
            P("dp", "head"),
            P("dp", "head"),
            P("dp", "head"),
            P("dp", "head"),
        ),
        check_vma=False,
    )
```

profile of v0, /device:TPU:48, one launch (start us, length us, event | category | flops | bytes accessed | tf_op | source)
XLA Modules:
  0.0 377.6 jit_solution(13306628696366333491)
XLA Ops:
  7.2 0.0 copy-start
  7.2 0.0 copy-start.6
  7.2 0.0 all-gather.2.cloned.1.call-start
  7.2 1.5 pad_maximum_fusion
  8.7 0.0 all-gather.2.cloned.1.call-update
  8.8 0.0 all-reduce.5.cloned.1.call-start
  8.8 1.2 copy.89
  10.1 0.8 convert_element_type.88
  10.9 1.8 copy.58
  12.7 0.1 copy.91
  12.8 1.2 copy.69
  14.0 0.1 fusion.15
  14.1 0.6 multiply_multiply_fusion
  14.7 0.2 fusion.41
  14.9 65.6 %all-gather.2.cloned.1.call-done = bf16[512,2048]{1,0:T(8,128)(2,1)} async-done(((bf16[16,2048]{1,0:T(8,128)(2,1)}), bf16[512,2048]{1,0:T(8,128)(2,1)}) %all-gather.2.cloned.1.call-update) | async-done | bytes 2097168 | tf_op jit(solution)/shard_map/all_gather | solution.py:89
  80.5 2.4 convolution_convert_fusion
  82.9 0.9 fusion.53
  83.8 0.2 copy.88
  84.0 0.0 copy-start.8
  84.0 0.5 fusion.55
  84.5 0.6 copy-done.8
  85.2 0.6 fusion.54
  85.8 0.3 fusion.6
  86.1 0.3 fusion.14
  86.4 2.1 copy.90
  88.4 2.3 convolution_bitcast_fusion
  90.8 2.6 copy.81
  93.3 1.7 multiply_reduce_fusion
  95.0 0.7 copy.82
  95.7 1.6 convolution_convert_fusion.1
  97.4 0.7 fusion.7
  98.1 0.3 copy-done.5
  98.4 0.5 convolution_convert_fusion.2
  98.9 0.5 copy-done.9
  99.3 1.1 convolution_bitcast_fusion.1
  100.5 1.6 fusion.8
  102.0 0.0 all-reduce.5.cloned.1.call-update
  102.1 1.3 dynamic-slice.4
  104.0 164.9 %all-reduce.5.cloned.1.call-done = (f32[256,64]{0,1:T(8,128)}, f32[256,512]{1,0:T(8,128)}) async-done(((f32[256,64]{0,1:T(8,128)}, f32[256,512]{1,0:T(8,128)}), (f32[256,64]{0,1:T(8,128)}, f32[256,512]{1,0:T(8,128)})) %all-reduce.5.cloned.1.call-update) | async-done | bytes 589840 | tf_op jit(solution)/shard_map/psum | solution.py:149
  268.8 1.2 fusion.22
  270.0 1.0 fusion.45
  271.0 0.1 copy.71
  271.1 0.1 copy.72
  271.3 1.3 fusion.21
  272.6 0.4 fusion.23
  273.0 54.6 %fusion = f32[24,448]{1,0:T(8,128)S(1)} fusion(f32[576,448]{1,0:T(8,128)S(1)} %fusion.23), kind=kCustom, calls=%all-reduce-scatter | all-reduce-scatter fusion | flops 344065 | bytes 1077248
  327.6 4.2 %collective-permute-start = (f32[24,448]{1,0:T(8,128)S(1)}, f32[24,448]{1,0:T(8,128)S(1)}, u32[]{:S(2)}, u32[]{:S(2)}) collective-permute-start(f32[24,448]{1,0:T(8,128)S(1)} %fusion), channel_id=1, source_target_pairs={{0,16},{16,32},{32,48},{48,64},{64,80},{80,96},{96,112},{112,128},... | collective-permute-start | bytes 129032
  331.8 6.7 %collective-permute-start.1 = (f32[24,448]{1,0:T(8,128)S(1)}, f32[24,448]{1,0:T(8,128)S(1)}, u32[]{:S(2)}, u32[]{:S(2)}) collective-permute-start(f32[24,448]{1,0:T(8,128)S(1)} %fusion), channel_id=1, source_target_pairs={{0,32},{16,48},{32,64},{48,80},{64,96},{80,112},{96,128},{112,144}... | collective-permute-start | bytes 129032
  338.5 1.9 collective-permute-start.7
  340.4 0.3 convolution_convert_fusion.3
  340.7 0.0 copy-start.14
  340.7 0.0 copy-start.15
  340.8 6.1 %collective-permute-start.2 = (f32[24,448]{1,0:T(8,128)S(1)}, f32[24,448]{1,0:T(8,128)S(1)}, u32[]{:S(2)}, u32[]{:S(2)}) collective-permute-start(f32[24,448]{1,0:T(8,128)S(1)} %fusion), channel_id=1, source_target_pairs={{0,48},{16,64},{32,80},{48,96},{64,112},{80,128},{96,144},{112,160... | collective-permute-start | bytes 129032
  346.9 2.2 collective-permute-start.3
  349.0 4.5 %collective-permute-start.4 = (f32[24,448]{1,0:T(8,128)S(1)}, f32[24,448]{1,0:T(8,128)S(1)}, u32[]{:S(2)}, u32[]{:S(2)}) collective-permute-start(f32[24,448]{1,0:T(8,128)S(1)} %fusion), channel_id=1, source_target_pairs={{0,80},{16,96},{32,112},{48,128},{64,144},{80,160},{96,176},{112,1... | collective-permute-start | bytes 129032
  353.5 2.7 collective-permute-start.5
  356.3 3.2 collective-permute-start.6
  359.5 0.3 convolution_convert_fusion.4
  359.8 1.0 copy.73
  360.8 0.8 copy.74
  361.7 0.9 collective-permute-done.5
  362.5 6.4 %collective-permute-done.6 = f32[24,448]{1,0:T(8,128)S(1)} collective-permute-done((f32[24,448]{1,0:T(8,128)S(1)}, f32[24,448]{1,0:T(8,128)S(1)}, u32[]{:S(2)}, u32[]{:S(2)}) %collective-permute-start.6) | collective-permute-done | bytes 43040
  368.9 1.1 concatenate.21
  370.0 0.7 multiply_subtract_fusion
  (56 shorter events, 0.2 us)
Async XLA Ops:
  7.2 265.4 %copy-start = (bf16[256,448]{0,1:T(8,128)(2,1)S(1)}, bf16[256,448]{0,1:T(8,128)(2,1)}, u32[]{:S(2)}) copy-start(bf16[256,448]{0,1:T(8,128)(2,1)} %param.12) | copy-start | bytes 688132
  7.2 5.5 %copy-start.13 = (bf16[256,1024]{1,0:T(8,128)(2,1)S(1)}, bf16[256,1024]{1,0:T(8,128)(2,1)}, u32[]{:S(2)}) copy-start(bf16[256,1024]{1,0:T(8,128)(2,1)} %param.20) | copy-start | bytes 1572868
  7.2 6.8 %copy-start.6 = (bf16[256,512]{1,0:T(8,128)(2,1)S(1)}, bf16[256,512]{1,0:T(8,128)(2,1)}, u32[]{:S(2)}) copy-start(bf16[256,512]{1,0:T(8,128)(2,1)} %param.13) | copy-start | bytes 786436
  7.2 73.3 %all-gather.2.cloned.1.call-start = ((), (), s32[]{:S(2)}) async-start(), calls=%async_computation | async-start | bytes 2162688 | tf_op jit(solution)/shard_map/all_gather | solution.py:89
  8.8 71.8 %copy-start.17 = (f32[512]{0:T(512)S(1)}, f32[512]{0:T(512)}, u32[]{:S(2)}) copy-start(f32[512]{0:T(512)} %param.15) | copy-start | bytes 6148
  8.8 260.1 %all-reduce.5.cloned.1.call-start = ((), (), s32[]{:S(2)}) async-start(), calls=%async_computation.1 | async-start | bytes 1179648 | tf_op jit(solution)/shard_map/psum | solution.py:149
  10.1 74.0 %copy-start.4 = (bf16[256,1024]{0,1:T(8,128)(2,1)}, bf16[256,1024]{0,1:T(8,128)(2,1)S(1)}, u32[]{:S(2)}) copy-start(bf16[256,1024]{0,1:T(8,128)(2,1)S(1)} %copy.89) | copy-start | bytes 1572868
  12.8 70.1 %copy-start.1 = (bf16[32,8,8,128]{3,2,1,0:T(8,128)(2,1)}, bf16[32,8,8,128]{3,2,1,0:T(8,128)(2,1)S(1)}, u32[]{:S(2)}) copy-start(bf16[32,8,8,128]{3,2,1,0:T(8,128)(2,1)S(1)} %copy.91) | copy-start | bytes 1572868
  13.9 69.9 %copy-start.25 = (f32[32]{0:T(128)}, f32[32]{0:T(128)S(1)}, u32[]{:S(2)}) copy-start(f32[32]{0:T(128)S(1)} %multiply_exponential_fusion) | copy-start | bytes 388
  13.9 69.8 %copy-start.22 = (f32[256]{0:T(256)}, f32[256]{0:T(256)S(1)}, u32[]{:S(2)}) copy-start(f32[256]{0:T(256)S(1)} %fusion.48) | copy-start | bytes 3076
  14.7 69.1 %copy-start.19 = (f32[256]{0:T(256)}, f32[256]{0:T(256)S(1)}, u32[]{:S(2)}) copy-start(f32[256]{0:T(256)S(1)} %get-tuple-element.32) | copy-start | bytes 3076
  84.0 1.7 copy-start.2
  84.0 1.1 copy-start.8
  95.7 1.6 copy-start.10
  95.7 1.6 copy-start.12
  95.7 1.6 copy-start.21
  97.3 1.0 copy-start.5
  98.4 0.9 copy-start.9
  98.4 2.0 copy-start.11
  100.4 168.4 %copy-start.7 = (bf16[256,512]{1,0:T(8,128)(2,1)S(1)}, bf16[256,512]{1,0:T(8,128)(2,1)}, u32[]{:S(2)}) copy-start(bf16[256,512]{1,0:T(8,128)(2,1)} %param.13) | copy-start | bytes 786436
  100.4 168.4 %copy-start.18 = (f32[512]{0:T(512)S(1)}, f32[512]{0:T(512)}, u32[]{:S(2)}) copy-start(f32[512]{0:T(512)} %param.15) | copy-start | bytes 6148
  100.4 169.6 %copy-start.23 = (f32[256]{0:T(256)S(1)}, f32[256]{0:T(256)}, u32[]{:S(2)}) copy-start(f32[256]{0:T(256)} %copy-done.22) | copy-start | bytes 3076
  100.4 169.6 %copy-start.26 = (f32[32]{0:T(128)S(1)}, f32[32]{0:T(128)}, u32[]{:S(2)}) copy-start(f32[32]{0:T(128)} %copy-done.25) | copy-start | bytes 388
  100.4 170.8 %copy-start.20 = (f32[256]{0:T(256)S(1)}, f32[256]{0:T(256)}, u32[]{:S(2)}) copy-start(f32[256]{0:T(256)} %copy-done.19) | copy-start | bytes 3076
  100.5 170.8 %copy-start.24 = (f32[256]{0:T(256)S(1)}, f32[256]{0:T(256)}, u32[]{:S(2)}) copy-start(f32[256]{0:T(256)} %get-tuple-element.31) | copy-start | bytes 3076
  271.3 69.1 %copy-start.3 = (bf16[256,1024]{0,1:T(8,128)(2,1)S(1)}, bf16[256,1024]{0,1:T(8,128)(2,1)}, u32[]{:S(2)}) copy-start(bf16[256,1024]{0,1:T(8,128)(2,1)} %copy-done.2) | copy-start | bytes 1572868
  327.6 25.9 %collective-permute-start = (f32[24,448]{1,0:T(8,128)S(1)}, f32[24,448]{1,0:T(8,128)S(1)}, u32[]{:S(2)}, u32[]{:S(2)}) collective-permute-start(f32[24,448]{1,0:T(8,128)S(1)} %fusion), channel_id=1, source_target_pairs={{0,16},{16,32},{32,48},{48,64},{64,80},{80,96},{96,112},{112,128},... | collective-permute-start | bytes 129032
  331.8 24.5 %collective-permute-start.1 = (f32[24,448]{1,0:T(8,128)S(1)}, f32[24,448]{1,0:T(8,128)S(1)}, u32[]{:S(2)}, u32[]{:S(2)}) collective-permute-start(f32[24,448]{1,0:T(8,128)S(1)} %fusion), channel_id=1, source_target_pairs={{0,32},{16,48},{32,64},{48,80},{64,96},{80,112},{96,128},{112,144}... | collective-permute-start | bytes 129032
  338.5 10.6 %collective-permute-start.7 = (f32[18,448]{1,0:T(8,128)S(1)}, f32[18,448]{1,0:T(8,128)S(1)}, u32[]{:S(2)}, u32[]{:S(2)}) collective-permute-start(f32[18,448]{1,0:T(8,128)S(1)} %slice.32), channel_id=1, source_target_pairs={{0,128},{16,144},{32,160},{48,176},{64,192},{80,208},{96,224},{112... | collective-permute-start | bytes 96776
  340.7 29.3 %copy-start.14 = (f32[18,448]{1,0:T(8,128)S(1)}, f32[18,448]{1,0:T(8,128)}, u32[]{:S(2)}) copy-start(f32[18,448]{1,0:T(8,128)} %param.21) | copy-start | bytes 96772
  340.7 29.3 %copy-start.15 = (f32[18,448]{1,0:T(8,128)S(1)}, f32[18,448]{1,0:T(8,128)}, u32[]{:S(2)}) copy-start(f32[18,448]{1,0:T(8,128)} %param.22) | copy-start | bytes 96772
  340.7 29.3 %copy-start.16 = (f32[18,448]{1,0:T(8,128)S(1)}, f32[18,448]{1,0:T(8,128)}, u32[]{:S(2)}) copy-start(f32[18,448]{1,0:T(8,128)} %param.23) | copy-start | bytes 96772
  340.8 20.9 %collective-permute-start.2 = (f32[24,448]{1,0:T(8,128)S(1)}, f32[24,448]{1,0:T(8,128)S(1)}, u32[]{:S(2)}, u32[]{:S(2)}) collective-permute-start(f32[24,448]{1,0:T(8,128)S(1)} %fusion), channel_id=1, source_target_pairs={{0,48},{16,64},{32,80},{48,96},{64,112},{80,128},{96,144},{112,160... | collective-permute-start | bytes 129032
  346.9 14.8 %collective-permute-start.3 = (f32[24,448]{1,0:T(8,128)S(1)}, f32[24,448]{1,0:T(8,128)S(1)}, u32[]{:S(2)}, u32[]{:S(2)}) collective-permute-start(f32[24,448]{1,0:T(8,128)S(1)} %fusion), channel_id=1, source_target_pairs={{0,64},{16,80},{32,96},{48,112},{64,128},{80,144},{96,160},{112,17... | collective-permute-start | bytes 129032
  349.0 12.7 %collective-permute-start.4 = (f32[24,448]{1,0:T(8,128)S(1)}, f32[24,448]{1,0:T(8,128)S(1)}, u32[]{:S(2)}, u32[]{:S(2)}) collective-permute-start(f32[24,448]{1,0:T(8,128)S(1)} %fusion), channel_id=1, source_target_pairs={{0,80},{16,96},{32,112},{48,128},{64,144},{80,160},{96,176},{112,1... | collective-permute-start | bytes 129032
  353.5 9.0 %collective-permute-start.5 = (f32[24,448]{1,0:T(8,128)S(1)}, f32[24,448]{1,0:T(8,128)S(1)}, u32[]{:S(2)}, u32[]{:S(2)}) collective-permute-start(f32[24,448]{1,0:T(8,128)S(1)} %fusion), channel_id=1, source_target_pairs={{0,96},{16,112},{32,128},{48,144},{64,160},{80,176},{96,192},{112,... | collective-permute-start | bytes 129032
  356.3 12.6 %collective-permute-start.6 = (f32[24,448]{1,0:T(8,128)S(1)}, f32[24,448]{1,0:T(8,128)S(1)}, u32[]{:S(2)}, u32[]{:S(2)}) collective-permute-start(f32[24,448]{1,0:T(8,128)S(1)} %fusion), channel_id=1, source_target_pairs={{0,112},{16,128},{32,144},{48,160},{64,176},{80,192},{96,208},{112... | collective-permute-start | bytes 129032
Sparse Core Ops, SparseCore 0:
  10.8 69.7 all-gather.1
  102.2 166.6 all-reduce.4
where the time goes:
time: 379 us; the launch traced here: 378 us
  waiting for transfers between devices  238 us (63%)
  blocking collectives  54.6 us (14%)
  starting transfers between devices  31.6 us (8%)
  local copies, waits for them, and re-layouts  16.6 us (4%)
  between operations  15.2 us (4%)
  matrix products  12.2 us (3%)
  other arithmetic  9.68 us (3%)
    psum x1, waiting for transfers between devices, local(): latent_sum, rope_sum = lax.psum((latent_part, rope_part), 'head')  165 us
    all_gather x1, waiting for transfers between devices, local(): full_rows = lax.all_gather(joined, 'dp', axis=0, tiled=True)  65.6 us
    unnamed x1, blocking collectives  54.6 us
    unnamed x8, starting transfers between devices  31.5 us
    unnamed x62, local copies, waits for them, and re-layouts  10.2 us
  transfers between devices with their start and end apart: 10, of which 4 were waited for; matrix products, arithmetic and copies ran while one was open for 3% of the time, Pallas kernels for 0%

commit v1 on v0

--- a/solution.py
+++ b/solution.py
@@ -86,7 +86,15 @@
     latent = (latent_in * inverse_rms * latent_norm_scale).astype(jnp.bfloat16)
     joined = jnp.concatenate((key_up_matrix, value_up_matrix), axis=1)
     split_at = head_count * nope_width
-    full_rows = lax.all_gather(joined, "dp", axis=0, tiled=True)
+    full_rows = jnp.concatenate(
+        lax.all_to_all(
+            jnp.stack(lax.axis_size("dp") * [joined], axis=0),
+            axis_name="dp",
+            split_axis=0,
+            concat_axis=0,
+        ),
+        axis=0,
+    )
     projected = jnp.dot(latent, full_rows, preferred_element_type=jnp.float32)
     key_nope = (
         projected[:, :split_at]

time: 379 us -> 366 us (0.966)
  waiting for transfers between devices: 238 us -> 215 us
  starting transfers between devices: 31.6 us -> 40.7 us
    all_gather x1 -> x0, waiting for transfers between devices: 65.6 us -> none  [local(): full_rows = lax.all_gather(joined, 'dp', axis=0, tiled=True)]
    all_to_all x0 -> x1, waiting for transfers between devices: none -> 41.4 us  [local(): lax.all_to_all(jnp.stack(lax.axis_size('dp') * [joined], axis=0), axis_na...]
    all_to_all x0 -> x1, starting transfers between devices: none -> 9.13 us  [local(): lax.all_to_all(jnp.stack(lax.axis_size('dp') * [joined], axis=0), axis_na...]
    unnamed x62 -> x64, local copies, waits for them, and re-layouts: 10.2 us -> 11 us
where the time goes in v1:
time: 366 us; the launch traced here: 365 us
  waiting for transfers between devices  215 us (59%)
  blocking collectives  54.6 us (15%)
  starting transfers between devices  40.7 us (11%)
  local copies, waits for them, and re-layouts  19.2 us (5%)
  between operations  15.2 us (4%)
  matrix products  11.7 us (3%)
  other arithmetic  9.19 us (3%)
    psum x1, waiting for transfers between devices, local(): latent_sum, rope_sum = lax.psum((latent_part, rope_part), 'head')  166 us
    unnamed x1, blocking collectives  54.6 us
    all_to_all x1, waiting for transfers between devices, local(): lax.all_to_all(jnp.stack(lax.axis_size('dp') * [joined], axis=0), axis_na...  41.4 us
    unnamed x8, starting transfers between devices  31.5 us
    unnamed x64, local copies, waits for them, and re-layouts  11 us
    all_to_all x1, starting transfers between devices, local(): lax.all_to_all(jnp.stack(lax.axis_size('dp') * [joined], axis=0), axis_na...  9.13 us
  transfers between devices with their start and end apart: 10, of which 4 were waited for; matrix products, arithmetic and copies ran while one was open for 3% of the time, Pallas kernels for 0%

profile of v1, /device:TPU:48, one launch (start us, length us, event | category | flops | bytes accessed | tf_op | source)
XLA Modules:
  0.0 365.3 jit_solution(2515973657941563254)
XLA Ops:
  7.2 0.0 copy-start
  7.2 0.8 pad_maximum_fusion
  8.0 1.6 stack.2
  9.6 9.1 %all-to-all-start = ((bf16[32,16,2048]{2,1,0:T(8,128)(2,1)}), bf16[32,16,2048]{2,1,0:T(8,128)(2,1)S(1)}, u32[]{:S(2)}, u32[]{:S(2)}) async-start(bf16[32,16,2048]{2,1,0:T(8,128)(2,1)} %stack.2), calls=%async_computation | async-start | bytes 4194304 | tf_op jit(solution)/shard_map/all_to_all | solution.py:90
  18.8 0.0 all-reduce.5.cloned.1.call-start
  18.8 0.2 copy.89
  19.1 2.0 copy.58
  21.0 1.1 copy.91
  22.2 1.2 copy.69
  23.3 0.0 copy-start.23
  23.4 1.1 fusion.15
  24.5 0.6 multiply_multiply_fusion
  25.1 0.2 fusion.41
  25.3 41.4 %all-to-all-done = bf16[32,16,2048]{2,1,0:T(8,128)(2,1)S(1)} async-done(((bf16[32,16,2048]{2,1,0:T(8,128)(2,1)}), bf16[32,16,2048]{2,1,0:T(8,128)(2,1)S(1)}, u32[]{:S(2)}, u32[]{:S(2)}) %all-to-all-start) | async-done | bytes 2097184 | tf_op jit(solution)/shard_map/all_to_all | solution.py:90
  66.7 1.9 convolution_convert_fusion
  68.5 1.1 fusion.53
  69.6 1.2 copy.88
  70.9 0.0 copy-start.9
  70.9 0.5 fusion.55
  71.4 0.6 copy-done.9
  72.0 0.6 fusion.54
  72.6 0.3 fusion.6
  72.9 0.3 fusion.14
  73.2 2.1 copy.90
  75.3 2.3 convolution_bitcast_fusion
  77.6 2.6 copy.81
  80.2 1.7 multiply_reduce_fusion
  81.9 0.7 copy.82
  82.5 1.6 convolution_convert_fusion.1
  84.2 0.7 fusion.7
  84.9 0.3 copy-done.7
  85.2 0.5 convolution_convert_fusion.2
  85.7 1.1 convolution_bitcast_fusion.1
  86.8 0.0 copy-done.2
  86.9 0.0 copy-start.25
  86.9 1.6 fusion.8
  88.4 0.0 all-reduce.5.cloned.1.call-update
  88.5 1.3 dynamic-slice.4
  90.4 166.2 %all-reduce.5.cloned.1.call-done = (f32[256,64]{0,1:T(8,128)}, f32[256,512]{1,0:T(8,128)}) async-done(((f32[256,64]{0,1:T(8,128)}, f32[256,512]{1,0:T(8,128)}), (f32[256,64]{0,1:T(8,128)}, f32[256,512]{1,0:T(8,128)})) %all-reduce.5.cloned.1.call-update) | async-done | bytes 589840 | tf_op jit(solution)/shard_map/psum | solution.py:157
  256.6 1.2 fusion.22
  257.8 1.0 fusion.45
  258.7 0.1 copy.71
  258.9 0.1 copy.72
  259.0 1.3 fusion.21
  260.3 0.4 fusion.23
  260.7 54.6 %fusion = f32[24,448]{1,0:T(8,128)S(1)} fusion(f32[576,448]{1,0:T(8,128)S(1)} %fusion.23), kind=kCustom, calls=%all-reduce-scatter | all-reduce-scatter fusion | flops 344065 | bytes 1077248
  315.3 4.2 %collective-permute-start = (f32[24,448]{1,0:T(8,128)S(1)}, f32[24,448]{1,0:T(8,128)S(1)}, u32[]{:S(2)}, u32[]{:S(2)}) collective-permute-start(f32[24,448]{1,0:T(8,128)S(1)} %fusion), channel_id=1, source_target_pairs={{0,16},{16,32},{32,48},{48,64},{64,80},{80,96},{96,112},{112,128},... | collective-permute-start | bytes 129032
  319.5 6.7 %collective-permute-start.1 = (f32[24,448]{1,0:T(8,128)S(1)}, f32[24,448]{1,0:T(8,128)S(1)}, u32[]{:S(2)}, u32[]{:S(2)}) collective-permute-start(f32[24,448]{1,0:T(8,128)S(1)} %fusion), channel_id=1, source_target_pairs={{0,32},{16,48},{32,64},{48,80},{64,96},{80,112},{96,128},{112,144}... | collective-permute-start | bytes 129032
  326.2 1.9 collective-permute-start.7
  328.1 0.3 convolution_convert_fusion.3
  328.4 0.0 copy-start.15
  328.5 0.0 copy-start.16
  328.5 6.1 %collective-permute-start.2 = (f32[24,448]{1,0:T(8,128)S(1)}, f32[24,448]{1,0:T(8,128)S(1)}, u32[]{:S(2)}, u32[]{:S(2)}) collective-permute-start(f32[24,448]{1,0:T(8,128)S(1)} %fusion), channel_id=1, source_target_pairs={{0,48},{16,64},{32,80},{48,96},{64,112},{80,128},{96,144},{112,160... | collective-permute-start | bytes 129032
  334.6 2.2 collective-permute-start.3
  336.7 4.5 %collective-permute-start.4 = (f32[24,448]{1,0:T(8,128)S(1)}, f32[24,448]{1,0:T(8,128)S(1)}, u32[]{:S(2)}, u32[]{:S(2)}) collective-permute-start(f32[24,448]{1,0:T(8,128)S(1)} %fusion), channel_id=1, source_target_pairs={{0,80},{16,96},{32,112},{48,128},{64,144},{80,160},{96,176},{112,1... | collective-permute-start | bytes 129032
  341.3 2.7 collective-permute-start.5
  344.0 3.2 collective-permute-start.6
  347.2 0.3 convolution_convert_fusion.4
  347.5 1.0 copy.73
  348.6 0.8 copy.74
  349.4 0.9 collective-permute-done.5
  350.3 6.4 %collective-permute-done.6 = f32[24,448]{1,0:T(8,128)S(1)} collective-permute-done((f32[24,448]{1,0:T(8,128)S(1)}, f32[24,448]{1,0:T(8,128)S(1)}, u32[]{:S(2)}, u32[]{:S(2)}) %collective-permute-start.6) | collective-permute-done | bytes 43040
  356.6 1.1 concatenate.21
  357.8 0.7 multiply_subtract_fusion
  (58 shorter events, 0.2 us)
Async XLA Ops:
  7.2 253.1 %copy-start = (bf16[256,448]{0,1:T(8,128)(2,1)S(1)}, bf16[256,448]{0,1:T(8,128)(2,1)}, u32[]{:S(2)}) copy-start(bf16[256,448]{0,1:T(8,128)(2,1)} %param.12) | copy-start | bytes 688132
  9.6 9.2 %copy-start.13 = (bf16[256,1024]{1,0:T(8,128)(2,1)S(1)}, bf16[256,1024]{1,0:T(8,128)(2,1)}, u32[]{:S(2)}) copy-start(bf16[256,1024]{1,0:T(8,128)(2,1)} %param.16) | copy-start | bytes 1572868
  9.6 9.4 %copy-start.17 = (bf16[256,64]{0,1:T(8,128)(2,1)S(1)}, bf16[256,64]{0,1:T(8,128)(2,1)}, u32[]{:S(2)}) copy-start(bf16[256,64]{0,1:T(8,128)(2,1)} %param.14) | copy-start | bytes 98308
  9.6 57.0 %all-to-all-start = ((bf16[32,16,2048]{2,1,0:T(8,128)(2,1)}), bf16[32,16,2048]{2,1,0:T(8,128)(2,1)S(1)}, u32[]{:S(2)}, u32[]{:S(2)}) async-start(bf16[32,16,2048]{2,1,0:T(8,128)(2,1)} %stack.2), calls=%async_computation | async-start | bytes 4194304 | tf_op jit(solution)/shard_map/all_to_all | solution.py:90
  18.7 47.9 %copy-start.18 = (f32[512]{0:T(512)S(1)}, f32[512]{0:T(512)}, u32[]{:S(2)}) copy-start(f32[512]{0:T(512)} %param.15) | copy-start | bytes 6148
  18.8 237.8 %all-reduce.5.cloned.1.call-start = ((), (), s32[]{:S(2)}) async-start(), calls=%async_computation.1 | async-start | bytes 1179648 | tf_op jit(solution)/shard_map/psum | solution.py:157
  19.0 51.8 %copy-start.6 = (bf16[256,1024]{0,1:T(8,128)(2,1)}, bf16[256,1024]{0,1:T(8,128)(2,1)S(1)}, u32[]{:S(2)}) copy-start(bf16[256,1024]{0,1:T(8,128)(2,1)S(1)} %copy.89) | copy-start | bytes 1572868
  22.2 46.4 %copy-start.3 = (bf16[32,8,8,128]{3,2,1,0:T(8,128)(2,1)}, bf16[32,8,8,128]{3,2,1,0:T(8,128)(2,1)S(1)}, u32[]{:S(2)}) copy-start(bf16[32,8,8,128]{3,2,1,0:T(8,128)(2,1)S(1)} %copy.91) | copy-start | bytes 1572868
  23.3 1.7 copy-start.26
  23.3 1.7 copy-start.23
  25.1 44.5 %copy-start.20 = (f32[256]{0:T(256)}, f32[256]{0:T(256)S(1)}, u32[]{:S(2)}) copy-start(f32[256]{0:T(256)S(1)} %get-tuple-element.32) | copy-start | bytes 3076
  66.7 2.9 copy-start.1
  70.8 1.7 copy-start.4
  70.9 1.1 copy-start.9
  82.5 1.6 copy-start.11
  82.5 1.6 copy-start.12
  82.5 1.6 copy-start.22
  84.2 1.0 copy-start.7
  84.2 1.5 copy-start.10
  85.2 1.6 copy-start.2
  86.8 169.7 %copy-start.8 = (bf16[256,512]{1,0:T(8,128)(2,1)S(1)}, bf16[256,512]{1,0:T(8,128)(2,1)}, u32[]{:S(2)}) copy-start(bf16[256,512]{1,0:T(8,128)(2,1)} %param.13) | copy-start | bytes 786436
  86.8 169.7 %copy-start.19 = (f32[512]{0:T(512)S(1)}, f32[512]{0:T(512)}, u32[]{:S(2)}) copy-start(f32[512]{0:T(512)} %param.15) | copy-start | bytes 6148
  86.8 170.9 %copy-start.24 = (f32[256]{0:T(256)S(1)}, f32[256]{0:T(256)}, u32[]{:S(2)}) copy-start(f32[256]{0:T(256)} %copy-done.23) | copy-start | bytes 3076
  86.8 170.9 %copy-start.27 = (f32[32]{0:T(128)S(1)}, f32[32]{0:T(128)}, u32[]{:S(2)}) copy-start(f32[32]{0:T(128)} %copy-done.26) | copy-start | bytes 388
  86.8 172.1 %copy-start.21 = (f32[256]{0:T(256)S(1)}, f32[256]{0:T(256)}, u32[]{:S(2)}) copy-start(f32[256]{0:T(256)} %copy-done.20) | copy-start | bytes 3076
  86.9 172.1 %copy-start.25 = (f32[256]{0:T(256)S(1)}, f32[256]{0:T(256)}, u32[]{:S(2)}) copy-start(f32[256]{0:T(256)} %get-tuple-element.31) | copy-start | bytes 3076
  259.0 69.1 %copy-start.5 = (bf16[256,1024]{0,1:T(8,128)(2,1)S(1)}, bf16[256,1024]{0,1:T(8,128)(2,1)}, u32[]{:S(2)}) copy-start(bf16[256,1024]{0,1:T(8,128)(2,1)} %copy-done.4) | copy-start | bytes 1572868
  315.3 26.0 %collective-permute-start = (f32[24,448]{1,0:T(8,128)S(1)}, f32[24,448]{1,0:T(8,128)S(1)}, u32[]{:S(2)}, u32[]{:S(2)}) collective-permute-start(f32[24,448]{1,0:T(8,128)S(1)} %fusion), channel_id=1, source_target_pairs={{0,16},{16,32},{32,48},{48,64},{64,80},{80,96},{96,112},{112,128},... | collective-permute-start | bytes 129032
  319.5 24.5 %collective-permute-start.1 = (f32[24,448]{1,0:T(8,128)S(1)}, f32[24,448]{1,0:T(8,128)S(1)}, u32[]{:S(2)}, u32[]{:S(2)}) collective-permute-start(f32[24,448]{1,0:T(8,128)S(1)} %fusion), channel_id=1, source_target_pairs={{0,32},{16,48},{32,64},{48,80},{64,96},{80,112},{96,128},{112,144}... | collective-permute-start | bytes 129032
  326.2 10.6 %collective-permute-start.7 = (f32[18,448]{1,0:T(8,128)S(1)}, f32[18,448]{1,0:T(8,128)S(1)}, u32[]{:S(2)}, u32[]{:S(2)}) collective-permute-start(f32[18,448]{1,0:T(8,128)S(1)} %slice.32), channel_id=1, source_target_pairs={{0,128},{16,144},{32,160},{48,176},{64,192},{80,208},{96,224},{112... | collective-permute-start | bytes 96776
  328.4 29.3 %copy-start.14 = (f32[18,448]{1,0:T(8,128)S(1)}, f32[18,448]{1,0:T(8,128)}, u32[]{:S(2)}) copy-start(f32[18,448]{1,0:T(8,128)} %param.21) | copy-start | bytes 96772
  328.4 29.3 %copy-start.15 = (f32[18,448]{1,0:T(8,128)S(1)}, f32[18,448]{1,0:T(8,128)}, u32[]{:S(2)}) copy-start(f32[18,448]{1,0:T(8,128)} %param.22) | copy-start | bytes 96772
  328.5 29.3 %copy-start.16 = (f32[18,448]{1,0:T(8,128)S(1)}, f32[18,448]{1,0:T(8,128)}, u32[]{:S(2)}) copy-start(f32[18,448]{1,0:T(8,128)} %param.23) | copy-start | bytes 96772
  328.5 20.9 %collective-permute-start.2 = (f32[24,448]{1,0:T(8,128)S(1)}, f32[24,448]{1,0:T(8,128)S(1)}, u32[]{:S(2)}, u32[]{:S(2)}) collective-permute-start(f32[24,448]{1,0:T(8,128)S(1)} %fusion), channel_id=1, source_target_pairs={{0,48},{16,64},{32,80},{48,96},{64,112},{80,128},{96,144},{112,160... | collective-permute-start | bytes 129032
  334.6 14.8 %collective-permute-start.3 = (f32[24,448]{1,0:T(8,128)S(1)}, f32[24,448]{1,0:T(8,128)S(1)}, u32[]{:S(2)}, u32[]{:S(2)}) collective-permute-start(f32[24,448]{1,0:T(8,128)S(1)} %fusion), channel_id=1, source_target_pairs={{0,64},{16,80},{32,96},{48,112},{64,128},{80,144},{96,160},{112,17... | collective-permute-start | bytes 129032
  336.7 12.7 %collective-permute-start.4 = (f32[24,448]{1,0:T(8,128)S(1)}, f32[24,448]{1,0:T(8,128)S(1)}, u32[]{:S(2)}, u32[]{:S(2)}) collective-permute-start(f32[24,448]{1,0:T(8,128)S(1)} %fusion), channel_id=1, source_target_pairs={{0,80},{16,96},{32,112},{48,128},{64,144},{80,160},{96,176},{112,1... | collective-permute-start | bytes 129032
  341.3 9.0 %collective-permute-start.5 = (f32[24,448]{1,0:T(8,128)S(1)}, f32[24,448]{1,0:T(8,128)S(1)}, u32[]{:S(2)}, u32[]{:S(2)}) collective-permute-start(f32[24,448]{1,0:T(8,128)S(1)} %fusion), channel_id=1, source_target_pairs={{0,96},{16,112},{32,128},{48,144},{64,160},{80,176},{96,192},{112,... | collective-permute-start | bytes 129032
  344.0 12.6 %collective-permute-start.6 = (f32[24,448]{1,0:T(8,128)S(1)}, f32[24,448]{1,0:T(8,128)S(1)}, u32[]{:S(2)}, u32[]{:S(2)}) collective-permute-start(f32[24,448]{1,0:T(8,128)S(1)} %fusion), channel_id=1, source_target_pairs={{0,112},{16,128},{32,144},{48,160},{64,176},{80,192},{96,208},{112... | collective-permute-start | bytes 129032
Sparse Core Ops, SparseCore 0:
  88.6 167.9 all-reduce.4
